TPU v7x, 128 devices: a whole 4x4x4 slice. The times are simulated.
128 devices in a mesh: row: 8 (over x_hi, z), col: 16 (over x_lo, y, core).
Axes of the slice: x: 4 (x_hi: 2, x_lo: 2; x = x_hi * 2 + x_lo), y: 4, z: 4, core: 2. Of those that a mesh axis runs over, the one named last changes fastest.
Arguments:
- tangents: float32 [3, 512, 512, 128], P(None, 'row', 'col'), may hold values from -400 to 400
- sea_mask: int32 [512, 512], P('row', 'col'), may hold values 0 or 1
- levels: int32 [512, 512], P('row', 'col'), may hold values from 0 to 49
- current: float32 [512, 512], P('row', 'col'), may hold values from -0.6 to 0.6
Outputs:
- new_tangents: float32 [3, 512, 512, 128], P(None, 'row', 'col')
- growth: float32 [128], replicated
All inputs are finite; a program needn't handle non-finite values. No bound on the sum of `sea_mask` on one device may be relied on, other than what follows from the above.
Results may differ from a plain program's by a relative error of at most 0.00014.
Values sent between devices are 32-bit elements; how exact they have to be, the bound alone decides.
A program may use at most 64 MiB of HBM per device.

v0:
```python
import jax
import jax.numpy as jnp
from jax import lax
from jax.sharding import PartitionSpec as P

STEPS = 2
RENORMS = 2
LEVELS = 50


viscosity = 0.15
gravity = 0.5
rotation = 0.4


def with_halo(cells, sides, width, closed):
    for axis, dim in sides:
        count = lax.axis_size(axis)
        ends = count if closed else count - 1
        head = lax.slice_in_dim(cells, 0, width, axis=dim)
        tail = lax.slice_in_dim(cells, cells.shape[dim] - width, cells.shape[dim], axis=dim)
        cells = jnp.concatenate(
            [
                lax.ppermute(tail, axis, [(i, (i + 1) % count) for i in range(ends)]),
                cells,
                lax.ppermute(head, axis, [((i + 1) % count, i) for i in range(ends)]),
            ],
            axis=dim,
        )
    return cells


def latitude_spin(first_row, row_count, total_rows):
    rows_global = first_row.astype(jnp.float32) + jnp.arange(row_count, dtype=jnp.float32)
    angle = (-70.0 + 140.0 * (rows_global + 0.5) / total_rows) * (jnp.pi / 180.0)
    return (rotation * jnp.sin(angle))[:, None, None]


def advance(padded, sea_frac, column_depth, current, coriolis):
    middle = padded[:, 1:-1, 1:-1]
    east_side = padded[:, 1:-1, 2:]
    west_side = padded[:, 1:-1, :-2]
    north_side = padded[:, 2:, 1:-1]
    south_side = padded[:, :-2, 1:-1]
    zonal_diff = 0.5 * (east_side - west_side)
    merid_diff = 0.5 * (north_side - south_side)
    spread = east_side + west_side + north_side + south_side - 4.0 * middle
    advected = middle + viscosity * spread - current * zonal_diff
    zonal = sea_frac * (advected[0] - gravity * zonal_diff[2] + coriolis * middle[1])
    meridional = sea_frac * (advected[1] - gravity * merid_diff[2] - coriolis * middle[0])
    height = sea_frac * (advected[2] - column_depth * (zonal_diff[0] + merid_diff[1]))
    return jnp.stack([zonal, meridional, height])


def body(tangents, sea_mask, levels, current):
    block_rows = tangents.shape[1]
    block_cols = tangents.shape[2]
    mode_count = tangents.shape[3]
    total_rows = block_rows * lax.axis_size("row")
    total_cells = block_rows * block_cols * lax.axis_size("row") * lax.axis_size("col")
    first_row = lax.axis_index("row") * block_rows
    sea_frac = sea_mask.astype(jnp.float32)
    column_depth = (levels + 1).astype(jnp.float32) / LEVELS
    inner_coefs = (
        sea_frac[:, :, None],
        column_depth[:, :, None],
        current[:, :, None],
        latitude_spin(first_row, block_rows, total_rows),
    )
    growth = jnp.zeros((mode_count,), jnp.float32)
    identity = jnp.eye(mode_count, dtype=jnp.float32)
    for renorm in range(RENORMS):
        for substep in range(STEPS):
            widened = with_halo(tangents, (("row", 1),), 1, False)
            widened = with_halo(widened, (("col", 2),), 1, True)
            tangents = advance(widened, *inner_coefs)
        flattened = tangents.reshape(-1, mode_count)
        partial_gram = (
            lax.dot_general(
                flattened, flattened, (((0,), (0,)), ((), ())), precision=lax.Precision.HIGHEST
            )
            / total_cells
        )
        gram_matrix = lax.psum(partial_gram, ("row", "col"))
        lower_factor = jnp.linalg.cholesky(gram_matrix)
        inverse_factor = jax.scipy.linalg.solve_triangular(lower_factor, identity, lower=True)
        tangents = jnp.dot(flattened, inverse_factor.T, precision=lax.Precision.HIGHEST).reshape(
            tangents.shape
        )
        growth = growth + jnp.log(jnp.diagonal(lower_factor))
    return (tangents, growth)


def solution(mesh):
    placed = (P(None, "row", "col", None), P("row", "col"), P("row", "col"), P("row", "col"))
    return jax.shard_map(
        body,
        mesh=mesh,
        in_specs=placed,
        out_specs=(P(None, "row", "col", None), P()),
        check_vma=False,
    )
```

profile of v0, /device:TPU:1, one launch (start us, length us, event | category | flops | bytes accessed | tf_op | source)
XLA Modules:
  0.0 478.9 jit_solution(10424090285825082650)
XLA Ops:
  9.3 5.0 %collective-permute-start = (f32[3,1,32,128]{3,1,2,0:T(1,128)S(1)}, f32[3,1,32,128]{3,1,2,0:T(1,128)S(1)}, u32[]{:S(2)}, u32[]{:S(2)}) collective-permute-start(f32[3,1,32,128]{3,1,2,0:T(1,128)S(1)} %bitcast.45), channel_id=1, source_target_pairs={{0,16},{16,32},{32,48},{48,64},{64,80},{80,96},{96,112},{1,17},{17... | collective-permute-start | bytes 147464 | tf_op jit(solution)/shard_map/ppermute | solution.py:24
  15.8 3.7 copy.26
  19.6 2.3 collective-permute-start.3
  23.6 2.7 collective-permute-done.2
  28.0 3.4 multiply_subtract_fusion.3
  33.3 3.5 collective-permute-start.4
  38.2 3.7 collective-permute-done.5
  45.8 1.9 collective-permute-done.6
  47.6 3.9 multiply_subtract_fusion.2
  51.5 1.9 broadcast_multiply_fusion.1
  54.8 5.9 %fusion.7 = f32[128,128]{0,1:T(8,128)} fusion(f32[1,64,32,128]{3,1,2,0:T(8,128)S(1)} %get-tuple-element.18, f32[1,64,32,128]{3,1,2,0:T(8,128)S(1)} %get-tuple-element.19, f32[1,64,32,128]{3,1,2,0:T(8,128)S(1)} %get-tuple-element.17), kind=kOutput, calls=%fused_computation.74 | convolution fusion | flops 1209548800 | bytes 3211264 | tf_op jit(solution)/shard_map/dot_general | solution.py:79
  62.9 148.4 %all-reduce.3.cloned.1.call-done = f32[128,128]{0,1:T(8,128)} async-done(((f32[128,128]{0,1:T(8,128)}), f32[128,128]{0,1:T(8,128)}) %all-reduce.3.cloned.1.call-update) | async-done | bytes 65552 | tf_op jit(solution)/shard_map/psum | solution.py:84
  213.2 11.7 %cholesky.44 = f32[128,128]{1,0:T(8,128)S(1)} custom-call(f32[128,128]{1,0:T(8,128)S(1)} %fusion.50), custom_call_target="Cholesky" | custom-call | tf_op jit(solution)/shard_map/jit(cholesky)/cholesky | solution.py:85
  226.2 9.8 %custom-call.10 = f32[1,128,128]{1,2,0:T(8,128)S(1)} custom-call(f32[1,128,128]{2,1,0:T(8,128)S(1)} %get-tuple-element.6), custom_call_target="InvertDiagBlocksLowerTriangular" | custom-call | tf_op jit(solution)/shard_map/jit(_solve_triangular)/triangular_solve | solution.py:86
  236.3 2.7 fusion.58
  239.1 2.0 copy.38
  241.2 3.0 collective-permute-start.8
  245.7 4.1 collective-permute-done.9
  252.1 2.4 collective-permute-done.10
  256.2 3.4 multiply_subtract_fusion.1
  259.7 1.9 fusion.25
  261.9 3.1 collective-permute-start.12
  267.6 2.5 collective-permute-done.13
  273.6 2.1 collective-permute-done.14
  275.7 3.8 multiply_subtract_fusion
  279.5 1.9 broadcast_multiply_fusion
  285.0 5.8 %fusion.6 = f32[128,128]{0,1:T(8,128)} fusion(f32[1,64,32,128]{3,1,2,0:T(8,128)S(1)} %get-tuple-element.12, f32[1,64,32,128]{3,1,2,0:T(8,128)S(1)} %get-tuple-element.13, f32[1,64,32,128]{3,1,2,0:T(8,128)S(1)} %get-tuple-element.11), kind=kOutput, calls=%fused_computation.72 | convolution fusion | flops 1209548800 | bytes 3211264 | tf_op jit(solution)/shard_map/dot_general | solution.py:79
  290.8 2.1 pad_maximum_fusion.51
  292.9 145.8 %all-reduce.5.cloned.1.call-done = f32[128,128]{0,1:T(8,128)} async-done(((f32[128,128]{0,1:T(8,128)}), f32[128,128]{0,1:T(8,128)}) %all-reduce.5.cloned.1.call-update) | async-done | bytes 65552 | tf_op jit(solution)/shard_map/psum | solution.py:84
  440.5 11.7 %cholesky.55 = f32[128,128]{1,0:T(8,128)S(1)} custom-call(f32[128,128]{1,0:T(8,128)S(1)} %fusion.48), custom_call_target="Cholesky" | custom-call | tf_op jit(solution)/shard_map/jit(cholesky)/cholesky | solution.py:85
  453.6 9.8 %custom-call.11 = f32[1,128,128]{1,2,0:T(8,128)S(1)} custom-call(f32[1,128,128]{2,1,0:T(8,128)S(1)} %get-tuple-element.4), custom_call_target="InvertDiagBlocksLowerTriangular" | custom-call | tf_op jit(solution)/shard_map/jit(_solve_triangular)/triangular_solve | solution.py:86
  465.1 6.2 %fusion = f32[3,64,32,128]{3,2,1,0:T(8,128)} fusion(f32[128,128,1,1]{1,0,3,2:T(8,128)S(1)} %convolution_bitcast_fusion, f32[3,64,32,128]{3,1,2,0:T(8,128)S(1)} %pad_maximum_fusion.51), kind=kOutput, calls=%fused_computation.54 | convolution fusion | flops 1207959552 | bytes 6356992 | tf_op jit(solution)/shard_map/dot_general | solution.py:87
  (72 shorter events, 41.9 us)
Async XLA Ops:
  7.2 204.2 %all-reduce.3.cloned.1.call-start = ((), (), s32[]{:S(2)}) async-start(), calls=%async_computation | async-start | bytes 131072 | tf_op jit(solution)/shard_map/psum | solution.py:84
  8.0 11.5 %collective-permute-start.1 = (f32[3,1,32,128]{3,1,2,0:T(1,128)S(1)}, f32[3,1,32,128]{3,1,2,0:T(1,128)S(1)}, u32[]{:S(2)}, u32[]{:S(2)}) collective-permute-start(f32[3,1,32,128]{3,1,2,0:T(1,128)S(1)} %bitcast.46), channel_id=1, source_target_pairs={{16,0},{32,16},{48,32},{64,48},{80,64},{96,80},{112,96},{17,1},{33... | collective-permute-start | bytes 147464 | tf_op jit(solution)/shard_map/ppermute | solution.py:26
  9.3 10.2 %collective-permute-start = (f32[3,1,32,128]{3,1,2,0:T(1,128)S(1)}, f32[3,1,32,128]{3,1,2,0:T(1,128)S(1)}, u32[]{:S(2)}, u32[]{:S(2)}) collective-permute-start(f32[3,1,32,128]{3,1,2,0:T(1,128)S(1)} %bitcast.45), channel_id=1, source_target_pairs={{0,16},{16,32},{32,48},{48,64},{64,80},{80,96},{96,112},{1,17},{17... | collective-permute-start | bytes 147464 | tf_op jit(solution)/shard_map/ppermute | solution.py:24
  15.8 3.7 copy-start.3
  19.6 4.1 collective-permute-start.3
  21.9 4.5 collective-permute-start.2
  33.3 4.9 %collective-permute-start.4 = (f32[3,1,32,128]{3,1,2,0:T(1,128)S(1)}, f32[3,1,32,128]{3,1,2,0:T(1,128)S(1)}, u32[]{:S(2)}, u32[]{:S(2)}) collective-permute-start(f32[3,1,32,128]{3,1,2,0:T(1,128)S(1)} %get-tuple-element.38), channel_id=1, source_target_pairs={{0,16},{16,32},{32,48},{48,64},{64,80},{80,96},{96,112},{1,17},{17... | collective-permute-start | bytes 147464 | tf_op jit(solution)/shard_map/ppermute | solution.py:24
  36.9 5.0 %collective-permute-start.5 = (f32[3,1,32,128]{3,1,2,0:T(1,128)S(1)}, f32[3,1,32,128]{3,1,2,0:T(1,128)S(1)}, u32[]{:S(2)}, u32[]{:S(2)}) collective-permute-start(f32[3,1,32,128]{3,1,2,0:T(1,128)S(1)} %get-tuple-element.39), channel_id=1, source_target_pairs={{16,0},{32,16},{48,32},{64,48},{80,64},{96,80},{112,96},{17,1},{33... | collective-permute-start | bytes 147464 | tf_op jit(solution)/shard_map/ppermute | solution.py:26
  41.9 3.8 collective-permute-start.7
  43.0 4.7 collective-permute-start.6
  60.7 378.1 %all-reduce.5.cloned.1.call-start = ((), (), s32[]{:S(2)}) async-start(), calls=%async_computation.1 | async-start | bytes 131072 | tf_op jit(solution)/shard_map/psum | solution.py:84
  241.2 4.5 collective-permute-start.8
  244.2 5.5 %collective-permute-start.9 = (f32[3,1,32,128]{3,1,2,0:T(1,128)S(1)}, f32[3,1,32,128]{3,1,2,0:T(1,128)S(1)}, u32[]{:S(2)}, u32[]{:S(2)}) collective-permute-start(f32[3,1,32,128]{3,1,2,0:T(1,128)S(1)} %get-tuple-element.37), channel_id=1, source_target_pairs={{16,0},{32,16},{48,32},{64,48},{80,64},{96,80},{112,96},{17,1},{33... | collective-permute-start | bytes 147464 | tf_op jit(solution)/shard_map/ppermute | solution.py:26
  249.8 2.4 collective-permute-start.11
  250.4 4.2 collective-permute-start.10
  261.9 5.7 %collective-permute-start.12 = (f32[3,1,32,128]{3,1,2,0:T(1,128)S(1)}, f32[3,1,32,128]{3,1,2,0:T(1,128)S(1)}, u32[]{:S(2)}, u32[]{:S(2)}) collective-permute-start(f32[3,1,32,128]{3,1,2,0:T(1,128)S(1)} %get-tuple-element.32), channel_id=1, source_target_pairs={{0,16},{16,32},{32,48},{48,64},{64,80},{80,96},{96,112},{1,17},{17... | collective-permute-start | bytes 147464 | tf_op jit(solution)/shard_map/ppermute | solution.py:24
  265.0 5.0 %collective-permute-start.13 = (f32[3,1,32,128]{3,1,2,0:T(1,128)S(1)}, f32[3,1,32,128]{3,1,2,0:T(1,128)S(1)}, u32[]{:S(2)}, u32[]{:S(2)}) collective-permute-start(f32[3,1,32,128]{3,1,2,0:T(1,128)S(1)} %get-tuple-element.33), channel_id=1, source_target_pairs={{16,0},{32,16},{48,32},{64,48},{80,64},{96,80},{112,96},{17,1},{33... | collective-permute-start | bytes 147464 | tf_op jit(solution)/shard_map/ppermute | solution.py:26
  270.1 3.5 collective-permute-start.15
  271.5 4.2 collective-permute-start.14
  283.3 1.0 copy-start
  283.3 1.3 copy-start.1
  283.3 1.7 copy-start.2
Sparse Core Ops, SparseCore 0:
  60.8 150.5 all-reduce.2
  291.0 147.7 all-reduce.4
where the time goes:
time: 484 us; the launch traced here: 479 us
  waiting for transfers between devices  317 us (65%)
  other arithmetic  83.1 us (17%)
  starting transfers between devices  27.9 us (6%)
  matrix products  21.2 us (4%)
  local copies, waits for them, and re-layouts  15 us (3%)
  between operations  14.7 us (3%)
    psum x2, waiting for transfers between devices, body(): gram_matrix = lax.psum(partial_gram, ('row', 'col'))  294 us
    another operation x6, other arithmetic, body(): lower_factor = jnp.linalg.cholesky(gram_matrix)  24.8 us
    another operation x4, other arithmetic, body(): jax.scipy.linalg.solve_triangular(lower_factor, identity, lower=True)  20.9 us
    ppermute x8, starting transfers between devices, with_halo(): lax.ppermute(tail, axis, [(i, (i + 1) % count) for i in range(ends)])  20 us
    ppermute x8, waiting for transfers between devices, with_halo(): lax.ppermute(head, axis, [((i + 1) % count, i) for i in range(ends)])  19.3 us
    sub x4, other arithmetic, advance(): advected = middle + viscosity * spread - current * zonal_diff  14.6 us
    dot_general x2, matrix products, body(): lax.dot_general(flattened, flattened, (((0,), (0,)), ((), ())), precision...  11.7 us
  transfers between devices with their start and end apart: 18, of which 12 were waited for; matrix products, arithmetic and copies ran while one was open for 3% of the time, Pallas kernels for 0%

commit v1 on v0

v1 whole, which is shorter than its diff:
```python
import jax
import jax.numpy as jnp
from jax import lax
from jax.experimental import pallas as pl
from jax.experimental.pallas import tpu as pltpu
from jax.sharding import PartitionSpec as P

MESH = pl.DeviceIdType.MESH
F32 = jnp.float32
BF16 = jnp.bfloat16
ROWS, COLS = 8, 16
LAT, LON, MODES = 64, 32, 128
LEVELS = 50
CELLS = 512 * 512
ANY = pl.BlockSpec(memory_space=pl.ANY)
VMEM = pl.BlockSpec(memory_space=pltpu.VMEM)


def vmem(*shape):
    return pltpu.VMEM(shape, F32)


def remote(src, dst, sems, k, dev):
    return pltpu.make_async_remote_copy(
        src_ref=src, dst_ref=dst, send_sem=sems.at[2 * k], recv_sem=sems.at[2 * k + 1], device_id=dev, device_id_type=MESH
    )


def at(row, col):
    return {"row": row, "col": col}


def shift(row, col, drow, dcol):
    return at(lax.rem(row + drow + ROWS, ROWS), lax.rem(col + dcol + COLS, COLS))


def inner_peer(row, col, d):
    member = lax.rem(lax.rem(col, 8) + d, 8)
    return member, at(row, (col // 8) * 8 + member)


def outer_index(row, col):
    return (col // 8) * 8 + row


def outer_peer(row, col, d):
    k = lax.rem(outer_index(row, col) + d, 16)
    return at(lax.rem(k, 8), (k // 8) * 8 + lax.rem(col, 8))


NEIGHBOURS = [(0, -1), (0, 1), (-1, 0), (1, 0), (-1, -1), (-1, 1), (1, -1), (1, 1)]


def greet(row, col, halo):
    barrier = pltpu.get_barrier_semaphore()
    peers = [inner_peer(row, col, d)[1] for d in range(1, 8)] + [outer_peer(row, col, d) for d in range(1, 16)]
    if halo:
        peers += [shift(row, col, a, b) for a, b in NEIGHBOURS]
    for dev in peers:
        pl.semaphore_signal(barrier, inc=1, device_id=dev, device_id_type=MESH)
    return lambda: pl.semaphore_wait(barrier, len(peers))


class Reduce:
    def __init__(self, row, col, g, inner, part, outer, total, sems):
        self.row, self.col = row, col
        self.g, self.inner, self.part, self.outer, self.total, self.sems = g, inner, part, outer, total, sems
        self.me = lax.rem(col, 8)
        self.waits = []

    def scatter(self):
        for d in range(1, 8):
            member, dev = inner_peer(self.row, self.col, d)
            remote(self.g.at[member], self.inner.at[d], self.sems, 0, dev).start()

    def exchange(self):
        w = remote(self.inner.at[pl.ds(1, 7)], self.inner.at[pl.ds(1, 7)], self.sems, 0, inner_peer(self.row, self.col, 1)[1])
        w.wait_recv()
        s = self.g[self.me]
        for d in range(1, 8):
            s = s + self.inner[d]
        self.part[...] = s
        k = outer_index(self.row, self.col)
        for d in range(1, 16):
            remote(self.part, self.outer.at[k], self.sems, 1, outer_peer(self.row, self.col, d)).start()
        self.outer[k] = s
        self.waits.append(w)

    def gather(self):
        w = remote(self.outer.at[pl.ds(0, 15)], self.outer.at[pl.ds(0, 15)], self.sems, 1, outer_peer(self.row, self.col, 1))
        w.wait_recv()
        t = self.outer[0]
        for e in range(1, 16):
            t = t + self.outer[e]
        self.total[self.me] = t
        for d in range(1, 8):
            remote(self.total.at[self.me], self.total.at[self.me], self.sems, 2, inner_peer(self.row, self.col, d)[1]).start()
        self.waits.append(w)

    def finish(self):
        w = remote(self.total.at[pl.ds(0, 7)], self.total.at[pl.ds(0, 7)], self.sems, 2, inner_peer(self.row, self.col, 1)[1])
        w.wait_recv()
        self.waits.append(w)
        for w in self.waits:
            w.wait_send()
        return self.total[...].reshape(MODES, MODES)


REDUCE_SCRATCH = [vmem(8, 16, 128), vmem(8, 16, 128), vmem(16, 128), vmem(16, 16, 128), vmem(8, 16, 128)]


def split(x):
    hi = x.astype(BF16)
    return hi, (x - hi.astype(F32)).astype(BF16)


def gram_of(x):
    hi, lo = split(x)
    return lax.dot_general(hi, jnp.concatenate([hi, lo], axis=1), (((0,), (0,)), ((), ())), preferred_element_type=F32)


def close_gram(acc):
    cross = acc[:, 128:]
    return (acc[:, :128] + cross + cross.T) * (1.0 / CELLS)


def weights_of(inverse):
    hi, lo = split(inverse)
    return jnp.concatenate(
        [jnp.concatenate([hi, hi], axis=1), jnp.concatenate([lo, jnp.zeros_like(lo)], axis=1)], axis=0
    )


def apply_inverse(x, weights):
    hi, lo = split(x)
    both = lax.dot_general(
        jnp.concatenate([hi, lo], axis=1), weights, (((1,), (1,)), ((), ())), preferred_element_type=F32
    )
    return both[:, :128] + both[:, 128:]


def model_step(src, src_row, dst, dst_row, planes, spin, plane_row, rows, starts):
    @pl.loop(0, rows)
    def _(i):
        r, p, o = src_row + i, plane_row + i, dst_row + i
        cor = jnp.broadcast_to(spin[pl.ds(p, 1), :], (8, 128))
        for s in starts:
            here = pl.ds(s, 8)
            sea, flow, deep = planes[0, p, here, :], planes[1, p, here, :], planes[2, p, here, :]
            mid = [src[q, r, here, :] for q in range(3)]
            east = [src[q, r, pl.ds(s + 1, 8), :] for q in range(3)]
            west = [src[q, r, pl.ds(s - 1, 8), :] for q in range(3)]
            north = [src[q, r + 1, here, :] for q in range(3)]
            south = [src[q, r - 1, here, :] for q in range(3)]
            along = [east[q] - west[q] for q in range(3)]
            moved = [
                0.4 * mid[q] + 0.15 * ((east[q] + west[q]) + (north[q] + south[q])) - flow * along[q] for q in range(3)
            ]
            dst[0, o, here, :] = sea * (moved[0] - 0.25 * along[2] + cor * mid[1])
            dst[1, o, here, :] = sea * (moved[1] - 0.25 * (north[2] - south[2]) - cor * mid[0])
            dst[2, o, here, :] = sea * (moved[2] - deep * (along[0] + (north[1] - south[1])))


OUTER_STARTS = (7, 15, 23, 31, 39)
INNER_STARTS = (8, 16, 24, 32)


def start_kernel(
    x_hbm, mask_ref, levels_ref, current_ref, c_hbm, gram_ref,
    x, y, planes, table, north_table, south_table, spin, acc,
    send_w, send_e, recv_w, recv_e, send_k, recv_k, ghost,
    g, inner, part, outer, total, sems, hsems, lsem,
):
    row, col = lax.axis_index("row"), lax.axis_index("col")
    load = pltpu.make_async_copy(x_hbm, x.at[:, pl.ds(2, LAT), pl.ds(8, LON), :], lsem.at[0])
    load.start()
    wait_barrier = greet(row, col, True)

    packed = jnp.concatenate(
        [
            mask_ref[...].astype(F32),
            0.5 * current_ref[...],
            0.5 * ((levels_ref[...] + 1).astype(F32) / LEVELS),
            jnp.zeros((LAT, 32), F32),
        ],
        axis=1,
    )
    turned = jnp.concatenate([packed, jnp.zeros((64, 128), F32)], axis=0).T
    for k in range(3):
        table[k, 8:40, :] = turned[32 * k : 32 * k + 32, :]
    lat = lax.broadcasted_iota(jnp.int32, (72, 128), 0) + row * LAT - 1
    angle = (-70.0 + 140.0 * (lat.astype(F32) + 0.5) / (ROWS * LAT)) * (jnp.pi / 180.0)
    spin[...] = 0.4 * jnp.sin(angle)

    def row_copies(e, src, off, k):
        width = slice(None) if off == 0 else pl.ds(8, LON)
        return [
            remote(src.at[:, pl.ds(off, 2), width, :], ghost.at[e, 1], hsems, k, shift(row, col, -1, 0)),
            remote(src.at[:, pl.ds(off + 62, 2), width, :], ghost.at[e, 0], hsems, k + 1, shift(row, col, 1, 0)),
        ]

    def pack():
        @pl.loop(0, 16)
        def _(j):
            for q in range(3):
                for m in range(4):
                    send_w[q, j, 2 * m : 2 * m + 2, :] = x[q, 4 * j + m + 2, 8:10, :]
                    send_e[q, j, 2 * m : 2 * m + 2, :] = x[q, 4 * j + m + 2, 38:40, :]

        for c, (i, j) in enumerate(((2, 8), (2, 39), (65, 8), (65, 39))):
            for q in range(3):
                send_k[c, q : q + 1, :] = x[q, i, j : j + 1, :]

    def side_copies(e, k):
        out = [
            remote(send_w, recv_e.at[e], hsems, k, shift(row, col, 0, -1)),
            remote(send_e, recv_w.at[e], hsems, k + 1, shift(row, col, 0, 1)),
        ]
        for c, (a, b) in enumerate(((-1, -1), (-1, 1), (1, -1), (1, 1))):
            out.append(remote(send_k.at[c], recv_k.at[e, 3 - c], hsems, k + 2 + c, shift(row, col, a, b)))
        return out

    def unpack(e):
        @pl.loop(0, 16)
        def _(j):
            for q in range(3):
                for m in range(4):
                    x[q, 4 * j + m + 2, 6:8, :] = recv_w[e, q, j, 2 * m : 2 * m + 2, :]
                    x[q, 4 * j + m + 2, 40:42, :] = recv_e[e, q, j, 2 * m : 2 * m + 2, :]

        for c, (i, j) in enumerate(((1, 7), (1, 40), (66, 7), (66, 40))):
            for q in range(3):
                x[q, i, j : j + 1, :] = recv_k[e, c, q : q + 1, :]

        x[:, 0:2, 8:40, :] = ghost[e, 0]
        x[:, 66:68, 8:40, :] = ghost[e, 1]

        @pl.when(row == 0)
        def _():
            x[:, 0:2, :, :] = jnp.zeros((3, 2, 48, 128), F32)

        @pl.when(row == ROWS - 1)
        def _():
            x[:, 66:68, :, :] = jnp.zeros((3, 2, 48, 128), F32)

    wait_barrier()
    tables = [
        remote(table.at[:, pl.ds(8, 8), :], table.at[:, pl.ds(40, 8), :], hsems, 8, shift(row, col, 0, -1)),
        remote(table.at[:, pl.ds(32, 8), :], table.at[:, pl.ds(0, 8), :], hsems, 9, shift(row, col, 0, 1)),
        remote(table.at[:, pl.ds(8, 32), :], north_table, hsems, 10, shift(row, col, -1, 0)),
        remote(table.at[:, pl.ds(8, 32), :], south_table, hsems, 11, shift(row, col, 1, 0)),
    ]
    first = row_copies(0, x_hbm, 0, 0)
    for copy in tables + first:
        copy.start()
    load.wait()
    pack()
    sides = side_copies(0, 2)
    for copy in sides:
        copy.start()

    def spread(k, tile):
        start = pl.multiple_of(8 * tile, 8)
        lanes = table[k, pl.ds(start, 8), :]
        for i in range(LAT):
            planes[k, i + 1, pl.ds(start, 8), :] = jnp.broadcast_to(lanes[:, i : i + 1], (8, 128))

    for k in range(3):
        @pl.loop(1, 5)
        def _(tile):
            spread(k, tile)

    for copy in tables:
        copy.wait()
    for k in range(3):
        @pl.loop(0, 2)
        def _(edge):
            spread(k, 5 * edge)

        for tile in range(4):
            planes[k, 65, 8 * tile + 8 : 8 * tile + 16, :] = jnp.broadcast_to(north_table[k, 8 * tile : 8 * tile + 8, 0:1], (8, 128))
            planes[k, 0, 8 * tile + 8 : 8 * tile + 16, :] = jnp.broadcast_to(south_table[k, 8 * tile : 8 * tile + 8, 63:64], (8, 128))

    @pl.when(row == 0)
    def _():
        planes[0, 0, :, :] = jnp.zeros((48, 128), F32)

    @pl.when(row == ROWS - 1)
    def _():
        planes[0, 65, :, :] = jnp.zeros((48, 128), F32)

    for copy in first + sides:
        copy.wait()
    unpack(0)
    model_step(x, 1, y, 0, planes, spin, 0, LAT + 2, OUTER_STARTS)
    model_step(y, 1, x, 2, planes, spin, 1, LAT, INNER_STARTS)

    acc[...] = jnp.zeros_like(acc)

    @pl.loop(0, 8)
    def _(j):
        for q in range(3):
            acc[...] += gram_of(x[q, pl.ds(8 * j + 2, 8), 8:40, :].reshape(256, 128))

    g[...] = close_gram(acc[...]).reshape(8, 16, 128)
    reduce = Reduce(row, col, g, inner, part, outer, total, sems)
    reduce.scatter()
    pack()
    halo = row_copies(1, x, 2, 12) + side_copies(1, 14)
    for copy in halo:
        copy.start()
    reduce.exchange()
    for copy in halo:
        copy.wait()
    unpack(1)
    model_step(x, 1, y, 0, planes, spin, 0, LAT + 2, OUTER_STARTS)
    reduce.gather()
    model_step(y, 1, x, 2, planes, spin, 1, LAT, INNER_STARTS)
    store = pltpu.make_async_copy(x.at[:, pl.ds(2, LAT), pl.ds(8, LON), :], c_hbm, lsem.at[0])
    store.start()
    gram_ref[...] = reduce.finish()
    store.wait()


def start(tangents, sea_mask, levels, current):
    return pl.pallas_call(
        start_kernel,
        out_shape=(jax.ShapeDtypeStruct(tangents.shape, F32), jax.ShapeDtypeStruct((MODES, MODES), F32)),
        in_specs=[ANY, VMEM, VMEM, VMEM],
        out_specs=(ANY, VMEM),
        scratch_shapes=[
            vmem(3, 68, 48, 128), vmem(3, 66, 48, 128), vmem(3, 66, 48, 128), vmem(3, 48, 128), vmem(3, 32, 128),
            vmem(3, 32, 128), vmem(72, 128), vmem(128, 256),
            vmem(3, 16, 8, 128), vmem(3, 16, 8, 128), vmem(2, 3, 16, 8, 128), vmem(2, 3, 16, 8, 128), vmem(4, 8, 128), vmem(2, 4, 8, 128),
            vmem(2, 2, 3, 2, LON, 128),
            *REDUCE_SCRATCH,
            pltpu.SemaphoreType.DMA((6,)), pltpu.SemaphoreType.DMA((40,)), pltpu.SemaphoreType.DMA((1,)),
        ],
        compiler_params=pltpu.CompilerParams(collective_id=0, has_side_effects=True, vmem_limit_bytes=48 * 2**20),
        name="start",
    )(tangents, sea_mask, levels, current)


def normalise_kernel(c_hbm, inverse_ref, b_hbm, gram_ref, x, acc, g, inner, part, outer, total, sems, lsem):
    row, col = lax.axis_index("row"), lax.axis_index("col")
    pieces = 8
    loads = [pltpu.make_async_copy(c_hbm.at[pl.ds(768 * k, 768)], x.at[pl.ds(768 * k, 768)], lsem.at[k]) for k in range(pieces)]
    stores = [pltpu.make_async_copy(x.at[pl.ds(768 * k, 768)], b_hbm.at[pl.ds(768 * k, 768)], lsem.at[k]) for k in range(pieces)]
    for copy in loads:
        copy.start()
    wait_barrier = greet(row, col, False)
    weights = weights_of(inverse_ref[...])
    acc[...] = jnp.zeros_like(acc)
    for k in range(pieces):
        loads[k].wait()

        @pl.loop(0, 3)
        def _(j):
            here = pl.ds(pl.multiple_of(768 * k + 256 * j, 256), 256)
            b = apply_inverse(x[here, :], weights)
            x[here, :] = b
            acc[...] += gram_of(b)

        stores[k].start()
    g[...] = close_gram(acc[...]).reshape(8, 16, 128)
    wait_barrier()
    reduce = Reduce(row, col, g, inner, part, outer, total, sems)
    reduce.scatter()
    reduce.exchange()
    reduce.gather()
    gram_ref[...] = reduce.finish()
    for copy in stores:
        copy.wait()


def normalise(state, inverse):
    return pl.pallas_call(
        normalise_kernel,
        out_shape=(jax.ShapeDtypeStruct(state.shape, F32), jax.ShapeDtypeStruct((MODES, MODES), F32)),
        in_specs=[ANY, VMEM],
        out_specs=(ANY, VMEM),
        scratch_shapes=[
            vmem(*state.shape), vmem(128, 256), *REDUCE_SCRATCH, pltpu.SemaphoreType.DMA((6,)), pltpu.SemaphoreType.DMA((8,))
        ],
        compiler_params=pltpu.CompilerParams(collective_id=1, has_side_effects=True, vmem_limit_bytes=16 * 2**20),
        name="normalise",
    )(state, inverse)


def factor(gram_blocks):
    sub = lax.broadcasted_iota(jnp.int32, (8, 128), 0)
    lane = lax.broadcasted_iota(jnp.int32, (8, 128), 1)
    w = list(gram_blocks)
    for k in range(MODES):
        b, s = divmod(k, 8)
        panel = w[b]
        column = jnp.broadcast_to(panel[:, k : k + 1], (8, 128))
        scale = jnp.broadcast_to((1.0 / column)[s : s + 1, :], (8, 128))
        here = lane == k
        pivot = jnp.where(here, scale, jnp.broadcast_to(panel[s : s + 1, :], (8, 128)) * scale)
        for j in range(b, 16):
            c = column if j == b else jnp.broadcast_to(w[j][:, k : k + 1], (8, 128))
            new = jnp.where(here, 0.0, w[j]) - c * pivot
            w[j] = jnp.where(sub > s, new, w[j]) if j == b else new
    diagonal = jnp.zeros((8, 128), F32)
    inverse = []
    for i in range(16):
        on = lane == sub + 8 * i
        pivots = jnp.where(on, w[i], 0.0)
        diagonal = diagonal + pivots
        root = lax.rsqrt(jnp.sum(pivots, axis=1, keepdims=True))
        inverse.append(jnp.where(lane < sub + 8 * i, w[i], jnp.where(on, 1.0, 0.0)) * root)
    return inverse, 0.5 * jnp.log(jnp.sum(diagonal, axis=0, keepdims=True))


def factor_kernel(gram_ref, inverse_ref, log_ref):
    inverse, logs = factor([gram_ref[8 * i : 8 * i + 8, :] for i in range(16)])
    for i in range(16):
        inverse_ref[8 * i : 8 * i + 8, :] = inverse[i]
    log_ref[...] = logs


def factorise(gram):
    return pl.pallas_call(
        factor_kernel,
        out_shape=(jax.ShapeDtypeStruct((MODES, MODES), F32), jax.ShapeDtypeStruct((1, MODES), F32)),
        name="factorise",
    )(gram)


def finish_kernel(b_ref, inverse_ref, out_ref):
    weights = weights_of(inverse_ref[...])

    @pl.loop(0, b_ref.shape[0] // 256)
    def _(j):
        here = pl.ds(pl.multiple_of(256 * j, 256), 256)
        out_ref[here, :] = apply_inverse(b_ref[here, :], weights)


def finish(state, inverse):
    rows = 768
    return pl.pallas_call(
        finish_kernel,
        out_shape=jax.ShapeDtypeStruct(state.shape, F32),
        grid=(state.shape[0] // rows,),
        in_specs=[pl.BlockSpec((rows, MODES), lambda i: (i, 0)), pl.BlockSpec((MODES, MODES), lambda i: (0, 0))],
        out_specs=pl.BlockSpec((rows, MODES), lambda i: (i, 0)),
        name="finish",
    )(state, inverse)


def body(tangents, sea_mask, levels, current):
    state, gram = start(tangents, sea_mask, levels, current)
    inverse, logs = factorise(gram)
    state, gram = normalise(state.reshape(-1, MODES), inverse)
    inverse, more = factorise(gram)
    out = finish(state, inverse)
    return out.reshape(tangents.shape), (logs + more)[0]


def solution(mesh):
    placed = (P(None, "row", "col", None), P("row", "col"), P("row", "col"), P("row", "col"))
    return jax.shard_map(
        body,
        mesh=mesh,
        in_specs=placed,
        out_specs=(P(None, "row", "col", None), P()),
        check_vma=False,
    )
```

time: 484 us -> 107 us (0.22)
  waiting for transfers between devices: 317 us -> 0 us
  Pallas kernels: 0 us -> 98.9 us
  other arithmetic: 83.1 us -> 0.51 us
  starting transfers between devices: 27.9 us -> 0 us
  matrix products: 21.2 us -> 0 us
  between operations: 14.7 us -> 0.67 us
  local copies, waits for them, and re-layouts: 15 us -> 6.12 us
    psum x2 -> x0, waiting for transfers between devices: 294 us -> none  [body(): gram_matrix = lax.psum(partial_gram, ('row', 'col'))]
    pallas_call x0 -> x5, Pallas kernels: none -> 98.9 us  [the longest x1 39.1 us: start(): pl.pallas_call(start_kernel, out_shape=(jax.ShapeDtypeStruct(tangents.sha...]
    another operation x14 -> x0, other arithmetic: 48.6 us -> none  [the longest x6 24.8 us: body(): lower_factor = jnp.linalg.cholesky(gram_matrix)]
    ppermute x16 -> x0, starting transfers between devices: 27.7 us -> none  [the longest x8 20 us: with_halo(): lax.ppermute(tail, axis, [(i, (i + 1) % count) for i in range(ends)])]
    ppermute x16 -> x0, waiting for transfers between devices: 22.7 us -> none  [the longest x8 19.3 us: with_halo(): lax.ppermute(head, axis, [((i + 1) % count, i) for i in range(ends)])]
    dot_general x4 -> x0, matrix products: 20.6 us -> none  [the longest x2 11.7 us: body(): lax.dot_general(flattened, flattened, (((0,), (0,)), ((), ())), precision...]
    mul x12 -> x0, other arithmetic: 16.8 us -> none  [the longest x4 7.08 us: advance(): zonal_diff = 0.5 * (east_side - west_side)]
    sub x4 -> x0, other arithmetic: 14.6 us -> none  [advance(): advected = middle + viscosity * spread - current * zonal_diff]
  transfers between devices with their start and end apart: 18 -> 0, of which waited for: 12 -> 0; matrix products, arithmetic and copies ran while one was open for 3% -> 0% of each run, Pallas kernels for 0% -> 0%
where the time goes in v1:
time: 107 us; the launch traced here: 106 us
  Pallas kernels  98.9 us (92%)
  local copies, waits for them, and re-layouts  6.12 us (6%)
    pallas_call x1, Pallas kernels, start(): pl.pallas_call(start_kernel, out_shape=(jax.ShapeDtypeStruct(tangents.sha...  39.1 us
    pallas_call x1, Pallas kernels, normalise(): pl.pallas_call(normalise_kernel, out_shape=(jax.ShapeDtypeStruct(state.sh...  26.2 us
    pallas_call x2, Pallas kernels, factorise(): pl.pallas_call(factor_kernel, out_shape=(jax.ShapeDtypeStruct((MODES, MOD...  24.8 us
    pallas_call x1, Pallas kernels, finish(): pl.pallas_call(finish_kernel, out_shape=jax.ShapeDtypeStruct(state.shape,...  8.72 us
    unnamed x15, local copies, waits for them, and re-layouts  6.12 us

profile of v1, /device:TPU:1, one launch (start us, length us, event | category | flops | bytes accessed | tf_op | source)
XLA Modules:
  0.0 106.2 jit_solution(14569990153723890073)
XLA Ops:
  0.6 0.8 copy.6.mask_ref
  1.4 0.8 copy.7.levels_ref
  2.2 0.8 copy.8.current_ref
  3.0 39.1 %start.1 = (f32[3,64,32,128]{3,2,1,0:T(8,128)S(1)}, f32[128,128]{1,0:T(8,128)S(1)}) custom-call(f32[3,64,32,128]{3,2,1,0:T(8,128)} %x_hbm.1, s32[64,32]{1,0:T(8,128)S(1)} %copy.6.mask_ref, s32[64,32]{1,0:T(8,128)S(1)} %copy.7.levels_ref, f32[64,32]{1,0:T(8,128)S(1)} %copy.8.current_ref), custom_call_target="tpu_custom_call" | custom-call | tf_op jit(solution)/shard_map/start/pallas_call | solution.py:326
  42.2 0.0 copy-start.2
  42.2 0.6 copy-done.2
  42.8 12.4 %factorise.2 = (f32[128,128]{1,0:T(8,128)}, f32[1,128]{1,0:T(1,128)}) custom-call(f32[128,128]{1,0:T(8,128)} %copy-done.2), custom_call_target="tpu_custom_call" | custom-call | tf_op jit(solution)/shard_map/factorise/pallas_call | solution.py:424
  55.2 0.0 copy-start.1
  55.2 0.8 copy-done.1
  56.0 26.2 %normalise.1 = (f32[6144,128]{1,0:T(8,128)S(1)}, f32[128,128]{1,0:T(8,128)S(1)}) custom-call(f32[6144,128]{1,0:T(8,128)S(1)} %bitcast.4, f32[128,128]{1,0:T(8,128)S(1)} %copy-done.1), custom_call_target="tpu_custom_call" | custom-call | tf_op jit(solution)/shard_map/normalise/pallas_call | solution.py:377
  82.3 0.0 copy-start
  82.3 1.6 %copy-done = f32[6144,128]{1,0:T(8,128)} copy-done((f32[6144,128]{1,0:T(8,128)}, f32[6144,128]{1,0:T(8,128)S(1)}, u32[]{:S(2)}) %copy-start) | copy-done | bytes 3145752
  83.9 0.0 copy-start.3
  83.9 0.6 copy-done.3
  84.5 12.4 %factorise.3 = (f32[128,128]{1,0:T(8,128)}, f32[1,128]{1,0:T(1,128)}) custom-call(f32[128,128]{1,0:T(8,128)} %copy-done.3), custom_call_target="tpu_custom_call" | custom-call | tf_op jit(solution)/shard_map/factorise/pallas_call | solution.py:424
  96.9 0.0 copy-start.4
  96.9 0.0 copy-start.5
  96.9 8.7 %finish.1 = f32[6144,128]{1,0:T(8,128)} custom-call(f32[6144,128]{1,0:T(8,128)} %copy-done, f32[128,128]{1,0:T(8,128)} %get-tuple-element.15.inverse_ref), custom_call_target="tpu_custom_call" | custom-call | tf_op jit(solution)/shard_map/finish/pallas_call | solution.py:442
  105.7 0.0 copy-done.4
  105.7 0.0 copy-done.5
  105.7 0.5 add_bitcast_fusion
Async XLA Ops:
  42.2 0.6 copy-start.2
  55.2 0.8 copy-start.1
  82.3 1.6 %copy-start = (f32[6144,128]{1,0:T(8,128)}, f32[6144,128]{1,0:T(8,128)S(1)}, u32[]{:S(2)}) copy-start(f32[6144,128]{1,0:T(8,128)S(1)} %get-tuple-element.13.b_ref) | copy-start | bytes 9437188
  83.9 0.6 copy-start.3
  96.9 8.7 %copy-start.4 = (f32[1,128]{1,0:T(1,128)S(1)}, f32[1,128]{1,0:T(1,128)}, u32[]{:S(2)}) copy-start(f32[1,128]{1,0:T(1,128)} %get-tuple-element.16) | copy-start | bytes 1540
  96.9 8.7 %copy-start.5 = (f32[1,128]{1,0:T(1,128)S(1)}, f32[1,128]{1,0:T(1,128)}, u32[]{:S(2)}) copy-start(f32[1,128]{1,0:T(1,128)} %get-tuple-element.17) | copy-start | bytes 1540

commit v2 on v1

--- a/solution.py
+++ b/solution.py
@@ -51,11 +51,10 @@
 NEIGHBOURS = [(0, -1), (0, 1), (-1, 0), (1, 0), (-1, -1), (-1, 1), (1, -1), (1, 1)]
 
 
-def greet(row, col, halo):
+def greet(row, col):
     barrier = pltpu.get_barrier_semaphore()
     peers = [inner_peer(row, col, d)[1] for d in range(1, 8)] + [outer_peer(row, col, d) for d in range(1, 16)]
-    if halo:
-        peers += [shift(row, col, a, b) for a, b in NEIGHBOURS]
+    peers += [shift(row, col, a, b) for a, b in NEIGHBOURS]
     for dev in peers:
         pl.semaphore_signal(barrier, inc=1, device_id=dev, device_id_type=MESH)
     return lambda: pl.semaphore_wait(barrier, len(peers))
@@ -137,6 +136,58 @@
         jnp.concatenate([hi, lo], axis=1), weights, (((1,), (1,)), ((), ())), preferred_element_type=F32
     )
     return both[:, :128] + both[:, 128:]
+
+
+def lanes(x, k):
+    return jnp.broadcast_to(x[:, k : k + 1], (8, 128))
+
+
+def sublanes(x, s):
+    return jnp.broadcast_to(x[s : s + 1, :], (8, 128))
+
+
+def factor(blocks):
+    sub = lax.broadcasted_iota(jnp.int32, (8, 128), 0)
+    lane = lax.broadcasted_iota(jnp.int32, (8, 128), 1)
+    below = [sub > s for s in range(8)]
+    w = list(blocks)
+    for b in range(16):
+        inside = (lane >= 8 * b) & (lane < 8 * b + 8)
+        p = w[b]
+        c = [lanes(p, 8 * b + m) for m in range(8)]
+        upper, scales, pivot_rows = {}, [], []
+        for s in range(8):
+            here = lane == 8 * b + s
+            scale = sublanes(1.0 / c[s], s)
+            column = jnp.where(below[s], c[s], 0.0)
+            for m in range(s + 1, 8):
+                upper[s, m] = sublanes(c[m], s)
+            for m in range(s + 1, 8):
+                c[m] = c[m] - column * (scale * upper[s, m])
+            row = jnp.where(here, 1.0, sublanes(p, s))
+            if s < 7:
+                p = jnp.where(here & below[s], 0.0, p) - column * (scale * row)
+            scales.append(scale)
+            pivot_rows.append(jnp.where(inside & (lane > 8 * b + s), 0.0, row))
+        w[b] = p
+        for j in range(b + 1, 16):
+            a = [lanes(w[j], 8 * b + m) for m in range(8)]
+            t = jnp.where(inside, 0.0, w[j])
+            for s in range(8):
+                multiplier = a[s] * scales[s]
+                for m in range(s + 1, 8):
+                    a[m] = a[m] - multiplier * upper[s, m]
+                t = t - multiplier * pivot_rows[s]
+            w[j] = t
+    diagonal = jnp.zeros((8, 128), F32)
+    inverse = []
+    for i in range(16):
+        on = lane == sub + 8 * i
+        pivots = jnp.where(on, w[i], 0.0)
+        diagonal = diagonal + pivots
+        root = lax.rsqrt(jnp.sum(pivots, axis=1, keepdims=True))
+        inverse.append(jnp.where(lane < sub + 8 * i, w[i], jnp.where(on, 1.0, 0.0)) * root)
+    return jnp.concatenate(inverse, axis=0), 0.5 * jnp.log(jnp.sum(diagonal, axis=0, keepdims=True))
 
 
 def model_step(src, src_row, dst, dst_row, planes, spin, plane_row, rows, starts):
@@ -166,15 +217,15 @@
 
 
 def start_kernel(
-    x_hbm, mask_ref, levels_ref, current_ref, c_hbm, gram_ref,
+    x_hbm, mask_ref, levels_ref, current_ref, b_hbm, gram_ref, logs_ref,
     x, y, planes, table, north_table, south_table, spin, acc,
     send_w, send_e, recv_w, recv_e, send_k, recv_k, ghost,
-    g, inner, part, outer, total, sems, hsems, lsem,
+    b, g, inner, part, outer, total, sems, g2, inner2, part2, outer2, total2, sems2, hsems, lsem,
 ):
     row, col = lax.axis_index("row"), lax.axis_index("col")
     load = pltpu.make_async_copy(x_hbm, x.at[:, pl.ds(2, LAT), pl.ds(8, LON), :], lsem.at[0])
     load.start()
-    wait_barrier = greet(row, col, True)
+    wait_barrier = greet(row, col)
 
     packed = jnp.concatenate(
         [
@@ -295,12 +346,14 @@
     model_step(x, 1, y, 0, planes, spin, 0, LAT + 2, OUTER_STARTS)
     model_step(y, 1, x, 2, planes, spin, 1, LAT, INNER_STARTS)
 
+    def chunk(h):
+        return jnp.concatenate([x[q, pl.ds(32 * h + 2, 32), 8:40, :].reshape(1024, MODES) for q in range(3)], axis=0)
+
     acc[...] = jnp.zeros_like(acc)
 
-    @pl.loop(0, 8)
-    def _(j):
-        for q in range(3):
-            acc[...] += gram_of(x[q, pl.ds(8 * j + 2, 8), 8:40, :].reshape(256, 128))
+    @pl.loop(0, 2)
+    def _(h):
+        acc[...] += gram_of(chunk(h))
 
     g[...] = close_gram(acc[...]).reshape(8, 16, 128)
     reduce = Reduce(row, col, g, inner, part, outer, total, sems)
@@ -316,146 +369,86 @@
     model_step(x, 1, y, 0, planes, spin, 0, LAT + 2, OUTER_STARTS)
     reduce.gather()
     model_step(y, 1, x, 2, planes, spin, 1, LAT, INNER_STARTS)
-    store = pltpu.make_async_copy(x.at[:, pl.ds(2, LAT), pl.ds(8, LON), :], c_hbm, lsem.at[0])
+    gram = reduce.finish()
+
+    inverse, logs = factor([gram[8 * i : 8 * i + 8, :] for i in range(16)])
+    logs_ref[...] = logs
+    weights = weights_of(inverse)
+    acc[...] = jnp.zeros_like(acc)
+
+    @pl.loop(0, 2)
+    def _(h):
+        normal = apply_inverse(chunk(h), weights)
+        for q in range(3):
+            b[q, pl.ds(32 * h, 32), :, :] = normal[1024 * q : 1024 * q + 1024, :].reshape(32, LON, MODES)
+        acc[...] += gram_of(normal)
+
+    store = pltpu.make_async_copy(b, b_hbm, lsem.at[0])
     store.start()
-    gram_ref[...] = reduce.finish()
+    g2[...] = close_gram(acc[...]).reshape(8, 16, 128)
+    second = Reduce(row, col, g2, inner2, part2, outer2, total2, sems2)
+    second.scatter()
+    second.exchange()
+    second.gather()
+    gram_ref[...] = second.finish()
     store.wait()
 
 
 def start(tangents, sea_mask, levels, current):
     return pl.pallas_call(
         start_kernel,
-        out_shape=(jax.ShapeDtypeStruct(tangents.shape, F32), jax.ShapeDtypeStruct((MODES, MODES), F32)),
+        out_shape=(
+            jax.ShapeDtypeStruct(tangents.shape, F32),
+            jax.ShapeDtypeStruct((MODES, MODES), F32),
+            jax.ShapeDtypeStruct((1, MODES), F32),
+        ),
         in_specs=[ANY, VMEM, VMEM, VMEM],
-        out_specs=(ANY, VMEM),
+        out_specs=(ANY, VMEM, VMEM),
         scratch_shapes=[
             vmem(3, 68, 48, 128), vmem(3, 66, 48, 128), vmem(3, 66, 48, 128), vmem(3, 48, 128), vmem(3, 32, 128),
             vmem(3, 32, 128), vmem(72, 128), vmem(128, 256),
             vmem(3, 16, 8, 128), vmem(3, 16, 8, 128), vmem(2, 3, 16, 8, 128), vmem(2, 3, 16, 8, 128), vmem(4, 8, 128), vmem(2, 4, 8, 128),
             vmem(2, 2, 3, 2, LON, 128),
-            *REDUCE_SCRATCH,
-            pltpu.SemaphoreType.DMA((6,)), pltpu.SemaphoreType.DMA((40,)), pltpu.SemaphoreType.DMA((1,)),
+            vmem(3, LAT, LON, MODES),
+            *REDUCE_SCRATCH, pltpu.SemaphoreType.DMA((6,)),
+            *REDUCE_SCRATCH, pltpu.SemaphoreType.DMA((6,)),
+            pltpu.SemaphoreType.DMA((40,)), pltpu.SemaphoreType.DMA((1,)),
         ],
         compiler_params=pltpu.CompilerParams(collective_id=0, has_side_effects=True, vmem_limit_bytes=48 * 2**20),
         name="start",
     )(tangents, sea_mask, levels, current)
 
 
-def normalise_kernel(c_hbm, inverse_ref, b_hbm, gram_ref, x, acc, g, inner, part, outer, total, sems, lsem):
-    row, col = lax.axis_index("row"), lax.axis_index("col")
-    pieces = 8
-    loads = [pltpu.make_async_copy(c_hbm.at[pl.ds(768 * k, 768)], x.at[pl.ds(768 * k, 768)], lsem.at[k]) for k in range(pieces)]
-    stores = [pltpu.make_async_copy(x.at[pl.ds(768 * k, 768)], b_hbm.at[pl.ds(768 * k, 768)], lsem.at[k]) for k in range(pieces)]
-    for copy in loads:
-        copy.start()
-    wait_barrier = greet(row, col, False)
-    weights = weights_of(inverse_ref[...])
-    acc[...] = jnp.zeros_like(acc)
-    for k in range(pieces):
-        loads[k].wait()
-
-        @pl.loop(0, 3)
-        def _(j):
-            here = pl.ds(pl.multiple_of(768 * k + 256 * j, 256), 256)
-            b = apply_inverse(x[here, :], weights)
-            x[here, :] = b
-            acc[...] += gram_of(b)
-
-        stores[k].start()
-    g[...] = close_gram(acc[...]).reshape(8, 16, 128)
-    wait_barrier()
-    reduce = Reduce(row, col, g, inner, part, outer, total, sems)
-    reduce.scatter()
-    reduce.exchange()
-    reduce.gather()
-    gram_ref[...] = reduce.finish()
-    for copy in stores:
-        copy.wait()
-
-
-def normalise(state, inverse):
-    return pl.pallas_call(
-        normalise_kernel,
-        out_shape=(jax.ShapeDtypeStruct(state.shape, F32), jax.ShapeDtypeStruct((MODES, MODES), F32)),
-        in_specs=[ANY, VMEM],
-        out_specs=(ANY, VMEM),
-        scratch_shapes=[
-            vmem(*state.shape), vmem(128, 256), *REDUCE_SCRATCH, pltpu.SemaphoreType.DMA((6,)), pltpu.SemaphoreType.DMA((8,))
-        ],
-        compiler_params=pltpu.CompilerParams(collective_id=1, has_side_effects=True, vmem_limit_bytes=16 * 2**20),
-        name="normalise",
-    )(state, inverse)
-
-
-def factor(gram_blocks):
-    sub = lax.broadcasted_iota(jnp.int32, (8, 128), 0)
-    lane = lax.broadcasted_iota(jnp.int32, (8, 128), 1)
-    w = list(gram_blocks)
-    for k in range(MODES):
-        b, s = divmod(k, 8)
-        panel = w[b]
-        column = jnp.broadcast_to(panel[:, k : k + 1], (8, 128))
-        scale = jnp.broadcast_to((1.0 / column)[s : s + 1, :], (8, 128))
-        here = lane == k
-        pivot = jnp.where(here, scale, jnp.broadcast_to(panel[s : s + 1, :], (8, 128)) * scale)
-        for j in range(b, 16):
-            c = column if j == b else jnp.broadcast_to(w[j][:, k : k + 1], (8, 128))
-            new = jnp.where(here, 0.0, w[j]) - c * pivot
-            w[j] = jnp.where(sub > s, new, w[j]) if j == b else new
-    diagonal = jnp.zeros((8, 128), F32)
-    inverse = []
-    for i in range(16):
-        on = lane == sub + 8 * i
-        pivots = jnp.where(on, w[i], 0.0)
-        diagonal = diagonal + pivots
-        root = lax.rsqrt(jnp.sum(pivots, axis=1, keepdims=True))
-        inverse.append(jnp.where(lane < sub + 8 * i, w[i], jnp.where(on, 1.0, 0.0)) * root)
-    return inverse, 0.5 * jnp.log(jnp.sum(diagonal, axis=0, keepdims=True))
-
-
-def factor_kernel(gram_ref, inverse_ref, log_ref):
-    inverse, logs = factor([gram_ref[8 * i : 8 * i + 8, :] for i in range(16)])
-    for i in range(16):
-        inverse_ref[8 * i : 8 * i + 8, :] = inverse[i]
-    log_ref[...] = logs
-
-
-def factorise(gram):
-    return pl.pallas_call(
-        factor_kernel,
-        out_shape=(jax.ShapeDtypeStruct((MODES, MODES), F32), jax.ShapeDtypeStruct((1, MODES), F32)),
-        name="factorise",
-    )(gram)
-
-
-def finish_kernel(b_ref, inverse_ref, out_ref):
-    weights = weights_of(inverse_ref[...])
-
-    @pl.loop(0, b_ref.shape[0] // 256)
-    def _(j):
-        here = pl.ds(pl.multiple_of(256 * j, 256), 256)
-        out_ref[here, :] = apply_inverse(b_ref[here, :], weights)
-
-
-def finish(state, inverse):
-    rows = 768
+def finish_kernel(b_ref, gram_ref, logs_ref, out_ref, growth_ref, weights):
+    @pl.when(pl.program_id(0) == 0)
+    def _():
+        inverse, logs = factor([gram_ref[8 * i : 8 * i + 8, :] for i in range(16)])
+        weights[...] = weights_of(inverse)
+        growth_ref[...] = logs_ref[...] + logs
+
+    out_ref[...] = apply_inverse(b_ref[...], weights[...])
+
+
+def finish(state, gram, logs):
+    rows = 1536
+    whole = lambda i: (0, 0)
     return pl.pallas_call(
         finish_kernel,
-        out_shape=jax.ShapeDtypeStruct(state.shape, F32),
+        out_shape=(jax.ShapeDtypeStruct(state.shape, F32), jax.ShapeDtypeStruct((1, MODES), F32)),
         grid=(state.shape[0] // rows,),
-        in_specs=[pl.BlockSpec((rows, MODES), lambda i: (i, 0)), pl.BlockSpec((MODES, MODES), lambda i: (0, 0))],
-        out_specs=pl.BlockSpec((rows, MODES), lambda i: (i, 0)),
+        in_specs=[
+            pl.BlockSpec((rows, MODES), lambda i: (i, 0)), pl.BlockSpec((MODES, MODES), whole), pl.BlockSpec((1, MODES), whole)
+        ],
+        out_specs=(pl.BlockSpec((rows, MODES), lambda i: (i, 0)), pl.BlockSpec((1, MODES), whole)),
+        scratch_shapes=[pltpu.VMEM((2 * MODES, 2 * MODES), BF16)],
         name="finish",
-    )(state, inverse)
+    )(state, gram, logs)
 
 
 def body(tangents, sea_mask, levels, current):
-    state, gram = start(tangents, sea_mask, levels, current)
-    inverse, logs = factorise(gram)
-    state, gram = normalise(state.reshape(-1, MODES), inverse)
-    inverse, more = factorise(gram)
-    out = finish(state, inverse)
-    return out.reshape(tangents.shape), (logs + more)[0]
+    state, gram, logs = start(tangents, sea_mask, levels, current)
+    out, growth = finish(state.reshape(-1, MODES), gram, logs)
+    return out.reshape(tangents.shape), growth[0]
 
 
 def solution(mesh):

time: 107 us -> 70.9 us (0.66)
  Pallas kernels: 98.9 us -> 64.8 us
    pallas_call x4 -> x1, Pallas kernels: 59.8 us -> 8.59 us  [finish(): pl.pallas_call(finish_kernel, out_shape=(jax.ShapeDtypeStruct(state.shape...]
    pallas_call x1, Pallas kernels: 39.1 us -> 56.2 us  [start(): pl.pallas_call(start_kernel, out_shape=(jax.ShapeDtypeStruct(tangents.sha...]
    unnamed x15 -> x9, local copies, waits for them, and re-layouts: 6.12 us -> 5.19 us
where the time goes in v2:
time: 70.9 us; the launch traced here: 70.6 us
  Pallas kernels  64.8 us (91%)
  local copies, waits for them, and re-layouts  5.19 us (7%)
    pallas_call x1, Pallas kernels, start(): pl.pallas_call(start_kernel, out_shape=(jax.ShapeDtypeStruct(tangents.sha...  56.2 us
    pallas_call x1, Pallas kernels, finish(): pl.pallas_call(finish_kernel, out_shape=(jax.ShapeDtypeStruct(state.shape...  8.59 us
    unnamed x9, local copies, waits for them, and re-layouts  5.19 us

profile of v2, /device:TPU:1, one launch (start us, length us, event | category | flops | bytes accessed | tf_op | source)
XLA Modules:
  0.0 70.6 jit_solution(6012030635314546113)
XLA Ops:
  0.6 0.8 %copy.6.mask_ref = s32[64,32]{1,0:T(8,128)S(1)} copy(s32[64,32]{0,1:T(8,128)} %param.5) | data formatting | bytes 16384 | tf_op args[1]
  1.4 0.8 %copy.7.levels_ref = s32[64,32]{1,0:T(8,128)S(1)} copy(s32[64,32]{0,1:T(8,128)} %param.6) | data formatting | bytes 16384 | tf_op args[2]
  2.2 0.8 %copy.8.current_ref = f32[64,32]{1,0:T(8,128)S(1)} copy(f32[64,32]{0,1:T(8,128)} %param.7) | data formatting | bytes 16384 | tf_op args[3]
  3.0 56.2 %start.1 = (f32[3,64,32,128]{3,2,1,0:T(8,128)S(1)}, f32[128,128]{1,0:T(8,128)S(1)}, f32[1,128]{1,0:T(1,128)S(1)}) custom-call(f32[3,64,32,128]{3,2,1,0:T(8,128)} %x_hbm.1, s32[64,32]{1,0:T(8,128)S(1)} %copy.6.mask_ref, s32[64,32]{1,0:T(8,128)S(1)} %copy.7.levels_ref, f32[64,32]{1,0:T(8,128)S(1)} %copy.8.current_ref), custom_call_target="tpu_custom_call" | custom-call | tf_op jit(solution)/shard_map/start/pallas_call | solution.py:398
  59.2 0.0 copy-start
  59.2 1.6 %copy-done = f32[3,64,32,128]{3,2,1,0:T(8,128)} copy-done((f32[3,64,32,128]{3,2,1,0:T(8,128)}, f32[3,64,32,128]{3,2,1,0:T(8,128)S(1)}, u32[]{:S(2)}) %copy-start) | copy-done | bytes 3145752
  60.8 0.0 copy-start.1
  60.8 0.6 copy-done.1
  61.5 0.0 copy-start.2
  61.5 0.5 copy-done.2
  62.0 8.6 %finish.1 = (f32[6144,128]{1,0:T(8,128)}, f32[1,128]{1,0:T(1,128)}) custom-call(f32[6144,128]{1,0:T(8,128)} %bitcast.3, f32[128,128]{1,0:T(8,128)} %copy-done.1, f32[1,128]{1,0:T(1,128)} %copy-done.2), custom_call_target="tpu_custom_call" | custom-call | tf_op jit(solution)/shard_map/finish/pallas_call | solution.py:435
Async XLA Ops:
  59.2 1.6 %copy-start = (f32[3,64,32,128]{3,2,1,0:T(8,128)}, f32[3,64,32,128]{3,2,1,0:T(8,128)S(1)}, u32[]{:S(2)}) copy-start(f32[3,64,32,128]{3,2,1,0:T(8,128)S(1)} %get-tuple-element.7) | copy-start | bytes 9437188
  60.8 0.6 copy-start.1
  61.5 0.5 copy-start.2

commit v3 on v2

--- a/solution.py
+++ b/solution.py
@@ -14,6 +14,7 @@
 CELLS = 512 * 512
 ANY = pl.BlockSpec(memory_space=pl.ANY)
 VMEM = pl.BlockSpec(memory_space=pltpu.VMEM)
+HBM = pl.BlockSpec(memory_space=pltpu.HBM)
 
 
 def vmem(*shape):
@@ -190,10 +191,11 @@
     return jnp.concatenate(inverse, axis=0), 0.5 * jnp.log(jnp.sum(diagonal, axis=0, keepdims=True))
 
 
-def model_step(src, src_row, dst, dst_row, planes, spin, plane_row, rows, starts):
-    @pl.loop(0, rows)
+def model_step(src, src_row, dst, dst_row, planes, spin, count, lat_of, starts):
+    @pl.loop(0, count)
     def _(i):
-        r, p, o = src_row + i, plane_row + i, dst_row + i
+        lat = lat_of(i)
+        r, p, o = src_row + lat, 1 + lat, dst_row + lat
         cor = jnp.broadcast_to(spin[pl.ds(p, 1), :], (8, 128))
         for s in starts:
             here = pl.ds(s, 8)
@@ -217,28 +219,17 @@
 
 
 def start_kernel(
-    x_hbm, mask_ref, levels_ref, current_ref, b_hbm, gram_ref, logs_ref,
-    x, y, planes, table, north_table, south_table, spin, acc,
+    x_hbm, fields_ref, b, gram_ref, logs_ref,
+    x, y, z, planes, table, north_table, south_table, spin, acc,
     send_w, send_e, recv_w, recv_e, send_k, recv_k, ghost,
-    b, g, inner, part, outer, total, sems, g2, inner2, part2, outer2, total2, sems2, hsems, lsem,
+    g, inner, part, outer, total, sems, g2, inner2, part2, outer2, total2, sems2, hsems, lsem,
 ):
     row, col = lax.axis_index("row"), lax.axis_index("col")
     load = pltpu.make_async_copy(x_hbm, x.at[:, pl.ds(2, LAT), pl.ds(8, LON), :], lsem.at[0])
     load.start()
     wait_barrier = greet(row, col)
 
-    packed = jnp.concatenate(
-        [
-            mask_ref[...].astype(F32),
-            0.5 * current_ref[...],
-            0.5 * ((levels_ref[...] + 1).astype(F32) / LEVELS),
-            jnp.zeros((LAT, 32), F32),
-        ],
-        axis=1,
-    )
-    turned = jnp.concatenate([packed, jnp.zeros((64, 128), F32)], axis=0).T
-    for k in range(3):
-        table[k, 8:40, :] = turned[32 * k : 32 * k + 32, :]
+    table[:, 8:40, 0:LAT] = fields_ref[...]
     lat = lax.broadcasted_iota(jnp.int32, (72, 128), 0) + row * LAT - 1
     angle = (-70.0 + 140.0 * (lat.astype(F32) + 0.5) / (ROWS * LAT)) * (jnp.pi / 180.0)
     spin[...] = 0.4 * jnp.sin(angle)
@@ -250,7 +241,7 @@
             remote(src.at[:, pl.ds(off + 62, 2), width, :], ghost.at[e, 0], hsems, k + 1, shift(row, col, 1, 0)),
         ]
 
-    def pack():
+    def pack(x):
         @pl.loop(0, 16)
         def _(j):
             for q in range(3):
@@ -271,7 +262,7 @@
             out.append(remote(send_k.at[c], recv_k.at[e, 3 - c], hsems, k + 2 + c, shift(row, col, a, b)))
         return out
 
-    def unpack(e):
+    def unpack_sides(e, x):
         @pl.loop(0, 16)
         def _(j):
             for q in range(3):
@@ -279,6 +270,7 @@
                     x[q, 4 * j + m + 2, 6:8, :] = recv_w[e, q, j, 2 * m : 2 * m + 2, :]
                     x[q, 4 * j + m + 2, 40:42, :] = recv_e[e, q, j, 2 * m : 2 * m + 2, :]
 
+    def unpack_rows(e, x):
         for c, (i, j) in enumerate(((1, 7), (1, 40), (66, 7), (66, 40))):
             for q in range(3):
                 x[q, i, j : j + 1, :] = recv_k[e, c, q : q + 1, :]
@@ -294,33 +286,46 @@
         def _():
             x[:, 66:68, :, :] = jnp.zeros((3, 2, 48, 128), F32)
 
-    wait_barrier()
+    def spread(k, tile):
+        start = pl.multiple_of(8 * tile, 8)
+        lanes = table[k, pl.ds(start, 8), :]
+        for i in range(LAT):
+            planes[k, i + 1, pl.ds(start, 8), :] = jnp.broadcast_to(lanes[:, i : i + 1], (8, 128))
+
+    def chunk(x, h):
+        return jnp.concatenate([x[q, pl.ds(32 * h + 2, 32), 8:40, :].reshape(1024, MODES) for q in range(3)], axis=0)
+
+    def inside(x, z):
+        model_step(x, 2, y, 1, planes, spin, LAT - 2, lambda i: i + 1, INNER_STARTS)
+        model_step(y, 1, z, 2, planes, spin, LAT - 4, lambda i: i + 2, INNER_STARTS)
+
+    def side_edges(x):
+        model_step(x, 2, y, 1, planes, spin, LAT - 2, lambda i: i + 1, (7, 33))
+
+    def other_edges(x, z):
+        model_step(x, 2, y, 1, planes, spin, 4, lambda i: i - 1 + 62 * (i // 2), OUTER_STARTS)
+        model_step(y, 1, z, 2, planes, spin, 4, lambda i: i + 60 * (i // 2), INNER_STARTS)
+        model_step(y, 1, z, 2, planes, spin, LAT - 4, lambda i: i + 2, (8, 32))
+
+    rows = row_copies(0, x_hbm, 0, 0)
+    sides = side_copies(0, 2)
     tables = [
         remote(table.at[:, pl.ds(8, 8), :], table.at[:, pl.ds(40, 8), :], hsems, 8, shift(row, col, 0, -1)),
         remote(table.at[:, pl.ds(32, 8), :], table.at[:, pl.ds(0, 8), :], hsems, 9, shift(row, col, 0, 1)),
         remote(table.at[:, pl.ds(8, 32), :], north_table, hsems, 10, shift(row, col, -1, 0)),
         remote(table.at[:, pl.ds(8, 32), :], south_table, hsems, 11, shift(row, col, 1, 0)),
     ]
-    first = row_copies(0, x_hbm, 0, 0)
-    for copy in tables + first:
-        copy.start()
-    load.wait()
-    pack()
-    sides = side_copies(0, 2)
-    for copy in sides:
-        copy.start()
-
-    def spread(k, tile):
-        start = pl.multiple_of(8 * tile, 8)
-        lanes = table[k, pl.ds(start, 8), :]
-        for i in range(LAT):
-            planes[k, i + 1, pl.ds(start, 8), :] = jnp.broadcast_to(lanes[:, i : i + 1], (8, 128))
-
     for k in range(3):
         @pl.loop(1, 5)
         def _(tile):
             spread(k, tile)
 
+    load.wait()
+    pack(x)
+    wait_barrier()
+    for copy in sides + tables + rows:
+        copy.start()
+    inside(x, z)
     for copy in tables:
         copy.wait()
     for k in range(3):
@@ -340,35 +345,40 @@
     def _():
         planes[0, 65, :, :] = jnp.zeros((48, 128), F32)
 
-    for copy in first + sides:
-        copy.wait()
-    unpack(0)
-    model_step(x, 1, y, 0, planes, spin, 0, LAT + 2, OUTER_STARTS)
-    model_step(y, 1, x, 2, planes, spin, 1, LAT, INNER_STARTS)
-
-    def chunk(h):
-        return jnp.concatenate([x[q, pl.ds(32 * h + 2, 32), 8:40, :].reshape(1024, MODES) for q in range(3)], axis=0)
-
+    for copy in sides:
+        copy.wait()
+    unpack_sides(0, x)
+    side_edges(x)
+    for copy in rows:
+        copy.wait()
+    unpack_rows(0, x)
+    other_edges(x, z)
+
+    pack(z)
+    rows = row_copies(1, z, 2, 12)
+    sides = side_copies(1, 14)
+    for copy in rows + sides:
+        copy.start()
     acc[...] = jnp.zeros_like(acc)
 
     @pl.loop(0, 2)
     def _(h):
-        acc[...] += gram_of(chunk(h))
+        acc[...] += gram_of(chunk(z, h))
 
     g[...] = close_gram(acc[...]).reshape(8, 16, 128)
     reduce = Reduce(row, col, g, inner, part, outer, total, sems)
     reduce.scatter()
-    pack()
-    halo = row_copies(1, x, 2, 12) + side_copies(1, 14)
-    for copy in halo:
-        copy.start()
+    inside(z, x)
     reduce.exchange()
-    for copy in halo:
-        copy.wait()
-    unpack(1)
-    model_step(x, 1, y, 0, planes, spin, 0, LAT + 2, OUTER_STARTS)
+    for copy in sides:
+        copy.wait()
+    unpack_sides(1, z)
+    side_edges(z)
+    for copy in rows:
+        copy.wait()
+    unpack_rows(1, z)
     reduce.gather()
-    model_step(y, 1, x, 2, planes, spin, 1, LAT, INNER_STARTS)
+    other_edges(z, x)
     gram = reduce.finish()
 
     inverse, logs = factor([gram[8 * i : 8 * i + 8, :] for i in range(16)])
@@ -378,23 +388,20 @@
 
     @pl.loop(0, 2)
     def _(h):
-        normal = apply_inverse(chunk(h), weights)
+        normal = apply_inverse(chunk(x, h), weights)
         for q in range(3):
             b[q, pl.ds(32 * h, 32), :, :] = normal[1024 * q : 1024 * q + 1024, :].reshape(32, LON, MODES)
         acc[...] += gram_of(normal)
 
-    store = pltpu.make_async_copy(b, b_hbm, lsem.at[0])
-    store.start()
     g2[...] = close_gram(acc[...]).reshape(8, 16, 128)
     second = Reduce(row, col, g2, inner2, part2, outer2, total2, sems2)
     second.scatter()
     second.exchange()
     second.gather()
     gram_ref[...] = second.finish()
-    store.wait()
-
-
-def start(tangents, sea_mask, levels, current):
+
+
+def start(tangents, fields):
     return pl.pallas_call(
         start_kernel,
         out_shape=(
@@ -402,51 +409,53 @@
             jax.ShapeDtypeStruct((MODES, MODES), F32),
             jax.ShapeDtypeStruct((1, MODES), F32),
         ),
-        in_specs=[ANY, VMEM, VMEM, VMEM],
-        out_specs=(ANY, VMEM, VMEM),
+        in_specs=[HBM, VMEM],
+        out_specs=(VMEM, VMEM, VMEM),
         scratch_shapes=[
-            vmem(3, 68, 48, 128), vmem(3, 66, 48, 128), vmem(3, 66, 48, 128), vmem(3, 48, 128), vmem(3, 32, 128),
+            vmem(3, 68, 48, 128), vmem(3, 66, 48, 128), vmem(3, 68, 48, 128), vmem(3, 66, 48, 128), vmem(3, 48, 128), vmem(3, 32, 128),
             vmem(3, 32, 128), vmem(72, 128), vmem(128, 256),
             vmem(3, 16, 8, 128), vmem(3, 16, 8, 128), vmem(2, 3, 16, 8, 128), vmem(2, 3, 16, 8, 128), vmem(4, 8, 128), vmem(2, 4, 8, 128),
             vmem(2, 2, 3, 2, LON, 128),
-            vmem(3, LAT, LON, MODES),
             *REDUCE_SCRATCH, pltpu.SemaphoreType.DMA((6,)),
             *REDUCE_SCRATCH, pltpu.SemaphoreType.DMA((6,)),
             pltpu.SemaphoreType.DMA((40,)), pltpu.SemaphoreType.DMA((1,)),
         ],
         compiler_params=pltpu.CompilerParams(collective_id=0, has_side_effects=True, vmem_limit_bytes=48 * 2**20),
         name="start",
-    )(tangents, sea_mask, levels, current)
-
-
-def finish_kernel(b_ref, gram_ref, logs_ref, out_ref, growth_ref, weights):
-    @pl.when(pl.program_id(0) == 0)
-    def _():
-        inverse, logs = factor([gram_ref[8 * i : 8 * i + 8, :] for i in range(16)])
-        weights[...] = weights_of(inverse)
-        growth_ref[...] = logs_ref[...] + logs
-
-    out_ref[...] = apply_inverse(b_ref[...], weights[...])
+    )(tangents, fields)
+
+
+def finish_kernel(b_ref, gram_ref, logs_ref, out_hbm, growth_ref, out, sems):
+    inverse, logs = factor([gram_ref[8 * i : 8 * i + 8, :] for i in range(16)])
+    weights = weights_of(inverse)
+    growth_ref[...] = logs_ref[...] + logs
+    rows = out.shape[0] // 4
+    copies = []
+    for k in range(4):
+        here = pl.ds(rows * k, rows)
+        out[here, :] = apply_inverse(b_ref[here, :], weights)
+        copies.append(pltpu.make_async_copy(out.at[here], out_hbm.at[here], sems.at[k]))
+        copies[-1].start()
+    for copy in copies:
+        copy.wait()
 
 
 def finish(state, gram, logs):
-    rows = 1536
-    whole = lambda i: (0, 0)
     return pl.pallas_call(
         finish_kernel,
         out_shape=(jax.ShapeDtypeStruct(state.shape, F32), jax.ShapeDtypeStruct((1, MODES), F32)),
-        grid=(state.shape[0] // rows,),
-        in_specs=[
-            pl.BlockSpec((rows, MODES), lambda i: (i, 0)), pl.BlockSpec((MODES, MODES), whole), pl.BlockSpec((1, MODES), whole)
-        ],
-        out_specs=(pl.BlockSpec((rows, MODES), lambda i: (i, 0)), pl.BlockSpec((1, MODES), whole)),
-        scratch_shapes=[pltpu.VMEM((2 * MODES, 2 * MODES), BF16)],
+        in_specs=[VMEM, VMEM, VMEM],
+        out_specs=(HBM, VMEM),
+        scratch_shapes=[vmem(*state.shape), pltpu.SemaphoreType.DMA((4,))],
+        compiler_params=pltpu.CompilerParams(vmem_limit_bytes=16 * 2**20),
         name="finish",
     )(state, gram, logs)
 
 
 def body(tangents, sea_mask, levels, current):
-    state, gram, logs = start(tangents, sea_mask, levels, current)
+    depth = (levels.T + 1).astype(F32) / LEVELS
+    fields = jnp.stack([sea_mask.T.astype(F32), 0.5 * current.T, 0.5 * depth])
+    state, gram, logs = start(tangents, fields)
     out, growth = finish(state.reshape(-1, MODES), gram, logs)
     return out.reshape(tangents.shape), growth[0]
 

time: 70.9 us -> 62 us (0.87)
  Pallas kernels: 64.8 us -> 59.5 us
  local copies, waits for them, and re-layouts: 5.19 us -> 0 us
  other arithmetic: 0 us -> 1.47 us
    unnamed x9 -> x0, local copies, waits for them, and re-layouts: 5.19 us -> none
    pallas_call x1, Pallas kernels: 56.2 us -> 52.7 us  [start(): pl.pallas_call(start_kernel, out_shape=(jax.ShapeDtypeStruct(tangents.sha...]
    pallas_call x1, Pallas kernels: 8.59 us -> 6.78 us  [finish(): pl.pallas_call(finish_kernel, out_shape=(jax.ShapeDtypeStruct(state.shape...]
    another operation x0 -> x3, other arithmetic: none -> 1.47 us  [body(): fields = jnp.stack([sea_mask.T.astype(F32), 0.5 * current.T, 0.5 * depth])]
where the time goes in v3:
time: 62 us; the launch traced here: 61.6 us
  Pallas kernels  59.5 us (96%)
  other arithmetic  1.47 us (2%)
  between operations  0.64 us (1%)
    pallas_call x1, Pallas kernels, start(): pl.pallas_call(start_kernel, out_shape=(jax.ShapeDtypeStruct(tangents.sha...  52.7 us
    pallas_call x1, Pallas kernels, finish(): pl.pallas_call(finish_kernel, out_shape=(jax.ShapeDtypeStruct(state.shape...  6.78 us
    another operation x3, other arithmetic, body(): fields = jnp.stack([sea_mask.T.astype(F32), 0.5 * current.T, 0.5 * depth])  1.47 us

profile of v3, /device:TPU:1, one launch (start us, length us, event | category | flops | bytes accessed | tf_op | source)
XLA Modules:
  0.0 61.6 jit_solution(17272840394555357516)
XLA Ops:
  0.6 0.7 %convert_bitcast_fusion = f32[1,32,64]{2,1,0:T(8,128)S(1)} fusion(s32[64,32]{0,1:T(8,128)} %param.5), kind=kLoop, calls=%fused_computation.3 | loop fusion | flops 2048 | bytes 16384 | tf_op jit(solution)/shard_map/stack | solution.py:457
  1.4 0.7 %multiply_bitcast_fusion = (f32[1,32,64]{2,1,0:T(8,128)S(1)}, f32[1,32,64]{2,1,0:T(8,128)S(1)}) fusion(s32[64,32]{0,1:T(8,128)} %param.6, f32[64,32]{0,1:T(8,128)} %param.7), kind=kLoop, calls=%fused_computation.1 | loop fusion | flops 8192 | bytes 32768 | tf_op jit(solution)/shard_map/stack | solution.py:457
  2.1 52.7 %start.1 = (f32[3,64,32,128]{3,2,1,0:T(8,128)S(1)}, f32[128,128]{1,0:T(8,128)S(1)}, f32[1,128]{1,0:T(1,128)S(1)}) custom-call(f32[3,64,32,128]{3,2,1,0:T(8,128)} %x_hbm.1, f32[3,32,64]{2,1,0:T(8,128)S(1)} %pad_maximum_fusion.fields_ref), custom_call_target="tpu_custom_call" | custom-call | tf_op jit(solution)/shard_map/start/pallas_call | solution.py:405
  54.8 6.8 %finish.1 = (f32[6144,128]{1,0:T(8,128)}, f32[1,128]{1,0:T(1,128)}) custom-call(f32[6144,128]{1,0:T(8,128)S(1)} %bitcast.15, f32[128,128]{1,0:T(8,128)S(1)} %get-tuple-element.8.gram_ref, f32[1,128]{1,0:T(1,128)S(1)} %get-tuple-element.9.logs_ref), custom_call_target="tpu_custom_call" | custom-call | tf_op jit(solution)/shard_map/finish/pallas_call | solution.py:444
  (1 shorter events, 0.0 us)

commit v4 on v3

--- a/solution.py
+++ b/solution.py
@@ -44,9 +44,15 @@
     return (col // 8) * 8 + row
 
 
-def outer_peer(row, col, d):
-    k = lax.rem(outer_index(row, col) + d, 16)
-    return at(lax.rem(k, 8), (k // 8) * 8 + lax.rem(col, 8))
+OUTER = [(1, 0, 2), (1, 0, 1), (1, 0, 3), (0, 1, 2), (1, 1, 2), (0, 0, 2), (1, 0, 0), (0, 1, 1), (0, 1, 3), (1, 1, 1), (1, 1, 3)]
+OUTER += [(0, 0, 1), (0, 0, 3), (0, 1, 0), (1, 1, 0)]
+INNER = (4, 5, 3, 6, 2, 7, 1)
+
+
+def outer_peer(row, col, step):
+    high, low, dz = step
+    x_high, z = lax.rem(row // 4 + high, 2), lax.rem(lax.rem(row, 4) + dz, 4)
+    return at(4 * x_high + z, 8 * lax.rem(col // 8 + low, 2) + lax.rem(col, 8))
 
 
 NEIGHBOURS = [(0, -1), (0, 1), (-1, 0), (1, 0), (-1, -1), (-1, 1), (1, -1), (1, 1)]
@@ -54,8 +60,8 @@
 
 def greet(row, col):
     barrier = pltpu.get_barrier_semaphore()
-    peers = [inner_peer(row, col, d)[1] for d in range(1, 8)] + [outer_peer(row, col, d) for d in range(1, 16)]
-    peers += [shift(row, col, a, b) for a, b in NEIGHBOURS]
+    peers = [shift(row, col, a, b) for a, b in NEIGHBOURS[::-1]]
+    peers += [outer_peer(row, col, step) for step in OUTER] + [inner_peer(row, col, d)[1] for d in INNER]
     for dev in peers:
         pl.semaphore_signal(barrier, inc=1, device_id=dev, device_id_type=MESH)
     return lambda: pl.semaphore_wait(barrier, len(peers))
@@ -69,7 +75,7 @@
         self.waits = []
 
     def scatter(self):
-        for d in range(1, 8):
+        for d in INNER:
             member, dev = inner_peer(self.row, self.col, d)
             remote(self.g.at[member], self.inner.at[d], self.sems, 0, dev).start()
 
@@ -81,19 +87,19 @@
             s = s + self.inner[d]
         self.part[...] = s
         k = outer_index(self.row, self.col)
-        for d in range(1, 16):
-            remote(self.part, self.outer.at[k], self.sems, 1, outer_peer(self.row, self.col, d)).start()
+        for step in OUTER:
+            remote(self.part, self.outer.at[k], self.sems, 1, outer_peer(self.row, self.col, step)).start()
         self.outer[k] = s
         self.waits.append(w)
 
     def gather(self):
-        w = remote(self.outer.at[pl.ds(0, 15)], self.outer.at[pl.ds(0, 15)], self.sems, 1, outer_peer(self.row, self.col, 1))
+        w = remote(self.outer.at[pl.ds(0, 15)], self.outer.at[pl.ds(0, 15)], self.sems, 1, outer_peer(self.row, self.col, OUTER[0]))
         w.wait_recv()
         t = self.outer[0]
         for e in range(1, 16):
             t = t + self.outer[e]
         self.total[self.me] = t
-        for d in range(1, 8):
+        for d in INNER:
             remote(self.total.at[self.me], self.total.at[self.me], self.sems, 2, inner_peer(self.row, self.col, d)[1]).start()
         self.waits.append(w)
 
@@ -219,17 +225,27 @@
 
 
 def start_kernel(
-    x_hbm, fields_ref, b, gram_ref, logs_ref,
-    x, y, z, planes, table, north_table, south_table, spin, acc,
+    x_hbm, mask_hbm, levels_hbm, current_hbm, b, gram_ref, logs_ref,
+    mask_in, levels_in, current_in, x, y, z, planes, table, north_table, south_table, spin, acc,
     send_w, send_e, recv_w, recv_e, send_k, recv_k, ghost,
     g, inner, part, outer, total, sems, g2, inner2, part2, outer2, total2, sems2, hsems, lsem,
 ):
     row, col = lax.axis_index("row"), lax.axis_index("col")
     load = pltpu.make_async_copy(x_hbm, x.at[:, pl.ds(2, LAT), pl.ds(8, LON), :], lsem.at[0])
+    fields = [
+        pltpu.make_async_copy(src, dst, lsem.at[k])
+        for k, (src, dst) in enumerate(((mask_hbm, mask_in), (levels_hbm, levels_in), (current_hbm, current_in)), 1)
+    ]
+    for copy in fields:
+        copy.start()
     load.start()
     wait_barrier = greet(row, col)
 
-    table[:, 8:40, 0:LAT] = fields_ref[...]
+    for copy in fields:
+        copy.wait()
+    table[0, 8:40, 0:LAT] = mask_in[...].astype(F32)
+    table[1, 8:40, 0:LAT] = 0.5 * current_in[...]
+    table[2, 8:40, 0:LAT] = 0.5 * ((levels_in[...] + 1).astype(F32) / LEVELS)
     lat = lax.broadcasted_iota(jnp.int32, (72, 128), 0) + row * LAT - 1
     angle = (-70.0 + 140.0 * (lat.astype(F32) + 0.5) / (ROWS * LAT)) * (jnp.pi / 180.0)
     spin[...] = 0.4 * jnp.sin(angle)
@@ -323,7 +339,7 @@
     load.wait()
     pack(x)
     wait_barrier()
-    for copy in sides + tables + rows:
+    for copy in sides[2:] + tables + sides[:2] + rows:
         copy.start()
     inside(x, z)
     for copy in tables:
@@ -357,7 +373,7 @@
     pack(z)
     rows = row_copies(1, z, 2, 12)
     sides = side_copies(1, 14)
-    for copy in rows + sides:
+    for copy in sides[2:] + rows:
         copy.start()
     acc[...] = jnp.zeros_like(acc)
 
@@ -368,16 +384,18 @@
     g[...] = close_gram(acc[...]).reshape(8, 16, 128)
     reduce = Reduce(row, col, g, inner, part, outer, total, sems)
     reduce.scatter()
+    for copy in sides[:2]:
+        copy.start()
     inside(z, x)
     reduce.exchange()
+    for copy in rows:
+        copy.wait()
+    reduce.gather()
     for copy in sides:
         copy.wait()
     unpack_sides(1, z)
     side_edges(z)
-    for copy in rows:
-        copy.wait()
     unpack_rows(1, z)
-    reduce.gather()
     other_edges(z, x)
     gram = reduce.finish()
 
@@ -401,7 +419,7 @@
     gram_ref[...] = second.finish()
 
 
-def start(tangents, fields):
+def start(tangents, *fields):
     return pl.pallas_call(
         start_kernel,
         out_shape=(
@@ -409,20 +427,21 @@
             jax.ShapeDtypeStruct((MODES, MODES), F32),
             jax.ShapeDtypeStruct((1, MODES), F32),
         ),
-        in_specs=[HBM, VMEM],
+        in_specs=[HBM] * 4,
         out_specs=(VMEM, VMEM, VMEM),
         scratch_shapes=[
+            pltpu.VMEM((LON, LAT), jnp.int32), pltpu.VMEM((LON, LAT), jnp.int32), vmem(LON, LAT),
             vmem(3, 68, 48, 128), vmem(3, 66, 48, 128), vmem(3, 68, 48, 128), vmem(3, 66, 48, 128), vmem(3, 48, 128), vmem(3, 32, 128),
             vmem(3, 32, 128), vmem(72, 128), vmem(128, 256),
             vmem(3, 16, 8, 128), vmem(3, 16, 8, 128), vmem(2, 3, 16, 8, 128), vmem(2, 3, 16, 8, 128), vmem(4, 8, 128), vmem(2, 4, 8, 128),
             vmem(2, 2, 3, 2, LON, 128),
             *REDUCE_SCRATCH, pltpu.SemaphoreType.DMA((6,)),
             *REDUCE_SCRATCH, pltpu.SemaphoreType.DMA((6,)),
-            pltpu.SemaphoreType.DMA((40,)), pltpu.SemaphoreType.DMA((1,)),
+            pltpu.SemaphoreType.DMA((40,)), pltpu.SemaphoreType.DMA((4,)),
         ],
         compiler_params=pltpu.CompilerParams(collective_id=0, has_side_effects=True, vmem_limit_bytes=48 * 2**20),
         name="start",
-    )(tangents, fields)
+    )(tangents, *fields)
 
 
 def finish_kernel(b_ref, gram_ref, logs_ref, out_hbm, growth_ref, out, sems):
@@ -453,9 +472,8 @@
 
 
 def body(tangents, sea_mask, levels, current):
-    depth = (levels.T + 1).astype(F32) / LEVELS
-    fields = jnp.stack([sea_mask.T.astype(F32), 0.5 * current.T, 0.5 * depth])
-    state, gram, logs = start(tangents, fields)
+    fields = [pltpu.with_memory_space_constraint(v.T, pltpu.HBM) for v in (sea_mask, levels, current)]
+    state, gram, logs = start(tangents, *fields)
     out, growth = finish(state.reshape(-1, MODES), gram, logs)
     return out.reshape(tangents.shape), growth[0]
 

time: 62 us -> 58.5 us (0.944)
  Pallas kernels: 59.5 us -> 57.7 us
  other arithmetic: 1.47 us -> 0 us
    pallas_call x1, Pallas kernels: 52.7 us -> 51 us  [start(): pl.pallas_call(start_kernel, out_shape=(jax.ShapeDtypeStruct(tangents.sha...]
    another operation x3 -> x0, other arithmetic: 1.47 us -> none  [body(): fields = jnp.stack([sea_mask.T.astype(F32), 0.5 * current.T, 0.5 * depth])]
where the time goes in v4:
time: 58.5 us; the launch traced here: 58.4 us
  Pallas kernels  57.7 us (99%)
  between operations  0.64 us (1%)
    pallas_call x1, Pallas kernels, start(): pl.pallas_call(start_kernel, out_shape=(jax.ShapeDtypeStruct(tangents.sha...  51 us
    pallas_call x1, Pallas kernels, finish(): pl.pallas_call(finish_kernel, out_shape=(jax.ShapeDtypeStruct(state.shape...  6.78 us

profile of v4, /device:TPU:1, one launch (start us, length us, event | category | flops | bytes accessed | tf_op | source)
XLA Modules:
  0.0 58.4 jit_solution(4992050563812581774)
XLA Ops:
  0.6 51.0 %start.1 = (f32[3,64,32,128]{3,2,1,0:T(8,128)S(1)}, f32[128,128]{1,0:T(8,128)S(1)}, f32[1,128]{1,0:T(1,128)S(1)}) custom-call(f32[3,64,32,128]{3,2,1,0:T(8,128)} %x_hbm.1, s32[32,64]{1,0:T(8,128)} %bitcast.7, s32[32,64]{1,0:T(8,128)} %bitcast.8, f32[32,64]{1,0:T(8,128)} %bitcast.9), custom_call_target="tpu_custom_call" | custom-call | tf_op jit(solution)/shard_map/start/pallas_call | solution.py:423
  51.6 6.8 %finish.1 = (f32[6144,128]{1,0:T(8,128)}, f32[1,128]{1,0:T(1,128)}) custom-call(f32[6144,128]{1,0:T(8,128)S(1)} %bitcast.6, f32[128,128]{1,0:T(8,128)S(1)} %get-tuple-element.8.gram_ref, f32[1,128]{1,0:T(1,128)S(1)} %get-tuple-element.9.logs_ref), custom_call_target="tpu_custom_call" | custom-call | tf_op jit(solution)/shard_map/finish/pallas_call | solution.py:463

commit v5 on v4

--- a/solution.py
+++ b/solution.py
@@ -342,6 +342,8 @@
     for copy in sides[2:] + tables + sides[:2] + rows:
         copy.start()
     inside(x, z)
+    middle = [z[q, 4:64, 16:32, :].reshape(960, MODES) for q in range(3)]
+    acc[...] = gram_of(jnp.concatenate(middle, axis=0))
     for copy in tables:
         copy.wait()
     for k in range(3):
@@ -373,18 +375,13 @@
     pack(z)
     rows = row_copies(1, z, 2, 12)
     sides = side_copies(1, 14)
-    for copy in sides[2:] + rows:
-        copy.start()
-    acc[...] = jnp.zeros_like(acc)
-
-    @pl.loop(0, 2)
-    def _(h):
-        acc[...] += gram_of(chunk(z, h))
-
+    frame = [z[q, 2:66, c : c + 8, :].reshape(512, MODES) for q in range(3) for c in (8, 32)]
+    frame += [z[q, r : r + 2, 16:32, :].reshape(32, MODES) for q in range(3) for r in (2, 64)]
+    acc[...] += gram_of(jnp.concatenate(frame, axis=0))
     g[...] = close_gram(acc[...]).reshape(8, 16, 128)
     reduce = Reduce(row, col, g, inner, part, outer, total, sems)
     reduce.scatter()
-    for copy in sides[:2]:
+    for copy in sides[2:] + rows + sides[:2]:
         copy.start()
     inside(z, x)
     reduce.exchange()

time: 58.5 us -> 58.4 us (level)
  no operation moved by 1% of the time
where the time goes in v5:
time: 58.4 us; the launch traced here: 58.2 us
  Pallas kernels  57.6 us (99%)
  between operations  0.64 us (1%)
    pallas_call x1, Pallas kernels, start(): pl.pallas_call(start_kernel, out_shape=(jax.ShapeDtypeStruct(tangents.sha...  50.8 us
    pallas_call x1, Pallas kernels, finish(): pl.pallas_call(finish_kernel, out_shape=(jax.ShapeDtypeStruct(state.shape...  6.78 us

profile of v5, /device:TPU:1, one launch (start us, length us, event | category | flops | bytes accessed | tf_op | source)
XLA Modules:
  0.0 58.2 jit_solution(16994455036300010565)
XLA Ops:
  0.6 50.8 %start.1 = (f32[3,64,32,128]{3,2,1,0:T(8,128)S(1)}, f32[128,128]{1,0:T(8,128)S(1)}, f32[1,128]{1,0:T(1,128)S(1)}) custom-call(f32[3,64,32,128]{3,2,1,0:T(8,128)} %x_hbm.1, s32[32,64]{1,0:T(8,128)} %bitcast.7, s32[32,64]{1,0:T(8,128)} %bitcast.8, f32[32,64]{1,0:T(8,128)} %bitcast.9), custom_call_target="tpu_custom_call" | custom-call | tf_op jit(solution)/shard_map/start/pallas_call | solution.py:420
  51.4 6.8 %finish.1 = (f32[6144,128]{1,0:T(8,128)}, f32[1,128]{1,0:T(1,128)}) custom-call(f32[6144,128]{1,0:T(8,128)S(1)} %bitcast.6, f32[128,128]{1,0:T(8,128)S(1)} %get-tuple-element.8.gram_ref, f32[1,128]{1,0:T(1,128)S(1)} %get-tuple-element.9.logs_ref), custom_call_target="tpu_custom_call" | custom-call | tf_op jit(solution)/shard_map/finish/pallas_call | solution.py:460
